TPU v7x, 512 devices: a whole 4x4x16 slice. The times are simulated.
512 devices in a mesh: dp: 32 (over z, x_hi), lon: 16 (over y, x_lo, core).
Axes of the slice: x: 4 (x_hi: 2, x_lo: 2; x = x_hi * 2 + x_lo), y: 4, z: 16, core: 2. Of those that a mesh axis runs over, the one named last changes fastest.
Arguments:
- fields: bfloat16 [32, 128, 48, 768], P('dp', 'lon'), may hold values from -6 to 6
- cotangent: bfloat16 [32, 128, 48, 768], P('dp', 'lon'), may hold values from -6 to 6
- first_weight: bfloat16 [2, 8, 96, 96], replicated, may hold values from -0.4375 to 0.4375
- second_weight: bfloat16 [2, 8, 96, 96], replicated, may hold values from -0.4375 to 0.4375
Outputs:
- layer_out: bfloat16 [32, 128, 48, 768], P('dp', 'lon')
- field_grad: bfloat16 [32, 128, 48, 768], P('dp', 'lon')
- first_grad: float32 [2, 8, 96, 96], replicated
- second_grad: float32 [2, 8, 96, 96], replicated
All inputs are finite; a program needn't handle non-finite values.
Results may differ from a plain program's by a relative error of at most 0.015.
Values may be sent and summed in bfloat16 or wider, within the bound.
A program may use at most 64 MiB of HBM per device.

v0:
```python
import math
import jax
import jax.numpy as jnp
from jax import lax
from jax.sharding import PartitionSpec as P

COEF = 0.7978845608028654
CUBIC = 0.044715


def gelu_value(inner):
    hyper = jnp.tanh(COEF * (inner + CUBIC * inner * inner * inner))
    return 0.5 * inner * (1.0 + hyper)


def gelu_slope(inner):
    hyper = jnp.tanh(COEF * (inner + CUBIC * inner * inner * inner))
    return 0.5 * (1.0 + hyper) + 0.5 * inner * (1.0 - hyper * hyper) * COEF * (
        1.0 + 3.0 * CUBIC * inner * inner
    )


def make_basis(length, count):
    cell_idx = jnp.arange(length, dtype=jnp.int32)
    mode_idx = jnp.arange(count, dtype=jnp.int32)
    product = cell_idx[:, None] * mode_idx[None, :] % length
    angle = product.astype(jnp.float32) * jnp.float32(2.0 * math.pi / length)
    return jnp.stack([jnp.cos(angle), -jnp.sin(angle)], axis=-1).astype(jnp.bfloat16)


def lat_apply(spec, table, lat_scale):
    return (
        jnp.einsum("kphc,phqj->kqjc", spec, table, preferred_element_type=jnp.float32) * lat_scale
    ).astype(jnp.bfloat16)


def forward_weight(weight):
    return jnp.stack([jnp.stack([weight[0], weight[1]]), jnp.stack([-weight[1], weight[0]])])


def adjoint_weight(weight):
    return jnp.stack([jnp.stack([weight[0], -weight[1]]), jnp.stack([weight[1], weight[0]])])


def block_product(spec, stacked):
    return jnp.einsum("kphbi,pqbij->kqhbj", spec, stacked, preferred_element_type=jnp.float32)


def block_adjoint(spec, stacked):
    return jnp.einsum("kphbj,pqbij->kqhbi", spec, stacked, preferred_element_type=jnp.float32)


def block_outer(left, right):
    pairs = jnp.einsum("kphbi,kqhbj->pqbij", left, right, preferred_element_type=jnp.float32)
    return jnp.stack([pairs[0, 0] + pairs[1, 1], pairs[0, 1] - pairs[1, 0]])


def on_device(fields, cotangent, first_weight, second_weight):
    cell_rows = fields[0]
    cot_rows = cotangent[0]
    lat_rows = cell_rows.shape[1]
    channels = cell_rows.shape[2]
    groups = first_weight.shape[1]
    group_width = first_weight.shape[2]
    lon_count = lax.axis_size("lon")
    total_cells = cell_rows.shape[0] * lon_count
    dft_basis = make_basis(total_cells, total_cells // 2)
    lat_basis = make_basis(lat_rows, lat_rows)
    cos_tab = lat_basis[:, :, 0]
    sin_tab = lat_basis[:, :, 1]
    lat_fwd_table = jnp.stack(
        [jnp.stack([cos_tab, sin_tab], axis=1), jnp.stack([-sin_tab, cos_tab], axis=1)], axis=0
    )
    lat_inv_table = jnp.stack(
        [jnp.stack([cos_tab.T, -sin_tab.T], axis=1), jnp.stack([sin_tab.T, cos_tab.T], axis=1)],
        axis=0,
    )
    norm_scale = 1.0 / math.sqrt(total_cells)
    lat_scale = 1.0 / math.sqrt(lat_rows)
    local_modes = cell_rows.shape[0] // 2
    mode_idx = lax.axis_index("lon") * local_modes + jnp.arange(local_modes, dtype=jnp.int32)
    mode_weight = jnp.where(mode_idx == 0, 1.0, 2.0).astype(jnp.bfloat16)[:, None, None, None]
    first_fwd = forward_weight(first_weight)
    second_fwd = forward_weight(second_weight)
    first_adj = adjoint_weight(first_weight)
    second_adj = adjoint_weight(second_weight)

    def local_dft(all_lines):
        return (
            jnp.einsum("whc,wkp->kphc", all_lines, dft_basis, preferred_element_type=jnp.float32)
            * norm_scale
        ).astype(jnp.bfloat16)

    def local_idft(all_modes):
        return (
            jnp.einsum("kphc,wkp->whc", all_modes, dft_basis, preferred_element_type=jnp.float32)
            * norm_scale
        ).astype(jnp.bfloat16)

    def lines_to_modes(all_lines):
        return lax.all_to_all(local_dft(all_lines), "lon", split_axis=0, concat_axis=3, tiled=True)

    def modes_to_lines(all_modes):
        return lax.all_to_all(local_idft(all_modes), "lon", split_axis=0, concat_axis=2, tiled=True)

    def to_spectrum(grid_rows):
        return lines_to_modes(
            lax.all_to_all(grid_rows, "lon", split_axis=2, concat_axis=0, tiled=True)
        )

    def to_cells(spec_rows):
        return modes_to_lines(
            lax.all_to_all(spec_rows, "lon", split_axis=3, concat_axis=0, tiled=True)
        )

    def split_groups(spec_rows):
        return spec_rows.reshape(local_modes, 2, lat_rows, groups, group_width)

    def join_groups(spec_rows):
        return spec_rows.astype(jnp.bfloat16).reshape(local_modes, 2, lat_rows, channels)

    lon_spec = to_spectrum(cell_rows)
    spectrum = split_groups(lat_apply(lon_spec, lat_fwd_table, lat_scale))
    inner = block_product(spectrum, first_fwd)
    act = gelu_value(inner).astype(jnp.bfloat16)
    mixed = join_groups(block_product(act, second_fwd)) * mode_weight
    mixed_lon = lat_apply(mixed, lat_inv_table, lat_scale)
    wave = to_cells(mixed_lon)
    dual_lon = to_spectrum(cot_rows)
    dual = split_groups(lat_apply(dual_lon, lat_fwd_table, lat_scale) * mode_weight)
    back = block_adjoint(dual, second_adj)
    pre = (back * gelu_slope(inner)).astype(jnp.bfloat16)
    back_spec = join_groups(block_adjoint(pre, first_adj))
    back_lon = lat_apply(back_spec, lat_inv_table, lat_scale)
    pull = to_cells(back_lon)
    layer_out = (cell_rows.astype(jnp.float32) + wave.astype(jnp.float32)).astype(jnp.bfloat16)
    field_grad = (cot_rows.astype(jnp.float32) + pull.astype(jnp.float32)).astype(jnp.bfloat16)
    sample_count = lax.axis_size("dp")
    second_term = block_outer(act, dual) / sample_count
    first_term = block_outer(spectrum, pre) / sample_count
    first_grad, second_grad = lax.psum((first_term, second_term), ("dp", "lon"))
    return (layer_out[None], field_grad[None], first_grad, second_grad)


def solution(mesh):
    placed = (P("dp", "lon", None, None), P("dp", "lon", None, None), P(), P())
    return jax.shard_map(
        on_device,
        mesh=mesh,
        in_specs=placed,
        out_specs=(P("dp", "lon", None, None), P("dp", "lon", None, None), P(), P()),
        check_vma=False,
    )
```

profile of v0, /device:TPU:1, one launch (start us, length us, event | category | flops | bytes accessed | tf_op | source)
XLA Modules:
  0.0 643.6 jit_solution(1187848861176454927)
XLA Ops:
  7.2 2.0 copy.123
  9.3 3.1 reshape.309
  12.4 11.0 %all-to-all-start = ((bf16[16,2,9216]{2,1,0:T(2,128)(2,1)}), bf16[16,2,9216]{2,1,0:T(2,128)(2,1)}, u32[]{:S(2)}, u32[]{:S(2)}) async-start(bf16[16,2,9216]{2,1,0:T(2,128)(2,1)} %reshape.309), calls=%async_computation | async-start | bytes 1179648 | tf_op jit(solution)/shard_map/all_to_all | solution.py:108
  23.3 1.1 copy.137
  24.6 3.1 reshape.317
  30.0 4.0 all-to-all-done
  34.1 5.2 all-to-all-start.4
  40.8 2.4 reshape.310
  43.2 1.0 copy.124
  44.3 1.0 copy.125
  45.8 1.4 copy.126
  47.2 3.1 reshape.311
  50.3 6.4 %all-to-all-start.1 = ((bf16[16,2,9216]{2,1,0:T(2,128)(2,1)}), bf16[16,2,9216]{2,1,0:T(2,128)(2,1)}, u32[]{:S(2)}, u32[]{:S(2)}) async-start(bf16[16,2,9216]{2,1,0:T(2,128)(2,1)} %reshape.311), calls=%async_computation.1 | async-start | bytes 1179648 | tf_op jit(solution)/shard_map/all_to_all | solution.py:101
  59.0 2.4 reshape.318
  61.5 1.0 copy.138
  62.6 1.0 copy.139
  64.0 1.4 copy.140
  65.4 3.1 reshape.319
  68.5 5.9 all-to-all-start.5
  74.9 1.1 maximum_bitcast_fusion.6
  76.0 1.1 maximum_bitcast_fusion.7
  77.1 2.4 reshape.312
  79.6 1.0 copy.127
  80.6 1.6 reshape.275
  83.4 1.6 all-to-all-done.5
  85.0 2.4 reshape.320
  87.5 2.2 copy.141
  89.7 2.9 reshape.288
  94.9 1.6 convolution_bitcast_fusion
  96.5 1.3 fusion.6
  100.2 1.1 copy.148
  101.3 3.1 reshape.321
  104.4 4.5 all-to-all-start.6
  108.9 1.7 fusion.37
  111.8 1.2 fusion.40
  113.5 2.2 copy.132
  115.7 4.1 reshape.313
  119.9 1.4 fusion.69
  121.4 5.8 all-to-all-start.2
  127.3 1.0 maximum_multiply_fusion
  129.2 1.8 reshape.322
  131.0 1.2 copy.149
  132.3 1.5 fusion.30
  133.8 1.8 copy.151
  135.6 3.1 reshape.323
  138.7 5.7 all-to-all-start.7
  144.4 2.4 reshape.314
  146.9 1.2 copy.133
  148.1 1.5 fusion.27
  149.6 1.8 copy.135
  151.4 3.1 reshape.315
  154.5 451.1 %all-reduce.3.cloned.1.call-done = (f32[2,8,96,96]{2,3,1,0:T(8,128)}, f32[2,8,96,96]{2,3,1,0:T(8,128)}) async-done(((f32[2,8,96,96]{2,3,1,0:T(8,128)}, f32[2,8,96,96]{2,3,1,0:T(8,128)}), (f32[2,8,96,96]{2,3,1,0:T(8,128)}, f32[2,8,96,96]{2,3,1,0:T(8,128)})) %all-reduce.3.cloned.1.call-update) | async-done | bytes 1179664 | tf_op jit(solution)/shard_map/psum | solution.py:141
  605.7 2.4 copy.158
  608.0 1.1 copy.159
  609.2 7.4 %all-to-all-start.3 = ((bf16[16,2,9216]{2,1,0:T(2,128)(2,1)}), bf16[16,2,9216]{2,1,0:T(2,128)(2,1)}, u32[]{:S(2)}, u32[]{:S(2)}) async-start(bf16[16,2,9216]{2,1,0:T(2,128)(2,1)} %reshape.315), calls=%async_computation.3 | async-start | bytes 1179648 | tf_op jit(solution)/shard_map/all_to_all | solution.py:104
  616.6 2.4 reshape.324
  619.4 1.8 copy.152
  621.2 2.2 reshape.269
  623.5 2.3 add_convert_fusion
  625.8 1.3 all-to-all-done.3
  627.1 2.4 reshape.316
  629.9 1.8 copy.136
  631.7 2.2 reshape.268
  634.0 2.3 add_convert_fusion.1
  (107 shorter events, 17.1 us)
Async XLA Ops:
  12.3 11.0 %copy-start = (bf16[1,8,48,768]{3,2,1,0:T(8,128)(2,1)S(1)}, bf16[1,8,48,768]{3,2,1,0:T(8,128)(2,1)}, u32[]{:S(2)}) copy-start(bf16[1,8,48,768]{3,2,1,0:T(8,128)(2,1)} %param.5) | copy-start | bytes 1769476
  12.4 21.7 %all-to-all-start = ((bf16[16,2,9216]{2,1,0:T(2,128)(2,1)}), bf16[16,2,9216]{2,1,0:T(2,128)(2,1)}, u32[]{:S(2)}, u32[]{:S(2)}) async-start(bf16[16,2,9216]{2,1,0:T(2,128)(2,1)} %reshape.309), calls=%async_computation | async-start | bytes 1179648 | tf_op jit(solution)/shard_map/all_to_all | solution.py:108
  24.6 15.4 %copy-start.21 = (bf16[2,8,96,96]{3,2,1,0:T(8,128)(2,1)S(1)}, bf16[2,8,96,96]{3,2,1,0:T(8,128)(2,1)}, u32[]{:S(2)}) copy-start(bf16[2,8,96,96]{3,2,1,0:T(8,128)(2,1)} %param.6) | copy-start | bytes 884740
  34.1 16.2 %all-to-all-start.4 = ((bf16[16,2,9216]{2,1,0:T(2,128)(2,1)}), bf16[16,2,9216]{2,1,0:T(2,128)(2,1)}, u32[]{:S(2)}, u32[]{:S(2)}) async-start(bf16[16,2,9216]{2,1,0:T(2,128)(2,1)} %reshape.317), calls=%async_computation.4 | async-start | bytes 1179648 | tf_op jit(solution)/shard_map/all_to_all | solution.py:108
  44.3 1.0 copy-start.14
  47.2 9.6 %copy-start.29 = (bf16[48,1,48]{2,0,1:T(8,128)(2,1)S(1)}, bf16[48,1,48]{2,0,1:T(8,128)(2,1)}, u32[]{:S(2)}) copy-start(bf16[48,1,48]{2,0,1:T(8,128)(2,1)} %get-tuple-element.48) | copy-start | bytes 13828
  47.2 9.6 %copy-start.30 = (bf16[48,1,48]{2,0,1:T(8,128)(2,1)S(1)}, bf16[48,1,48]{2,0,1:T(8,128)(2,1)}, u32[]{:S(2)}) copy-start(bf16[48,1,48]{2,0,1:T(8,128)(2,1)} %get-tuple-element.49) | copy-start | bytes 13828
  47.2 9.6 %copy-start.31 = (bf16[48,1,48]{2,0,1:T(8,128)(2,1)S(1)}, bf16[48,1,48]{2,0,1:T(8,128)(2,1)}, u32[]{:S(2)}) copy-start(bf16[48,1,48]{2,0,1:T(8,128)(2,1)} %fusion.91) | copy-start | bytes 13828
  47.2 10.2 %copy-start.22 = (bf16[2,8,96,96]{3,2,1,0:T(8,128)(2,1)S(1)}, bf16[2,8,96,96]{3,2,1,0:T(8,128)(2,1)}, u32[]{:S(2)}) copy-start(bf16[2,8,96,96]{3,2,1,0:T(8,128)(2,1)} %param.7) | copy-start | bytes 884740
  50.3 18.2 %all-to-all-start.1 = ((bf16[16,2,9216]{2,1,0:T(2,128)(2,1)}), bf16[16,2,9216]{2,1,0:T(2,128)(2,1)}, u32[]{:S(2)}, u32[]{:S(2)}) async-start(bf16[16,2,9216]{2,1,0:T(2,128)(2,1)} %reshape.311), calls=%async_computation.1 | async-start | bytes 1179648 | tf_op jit(solution)/shard_map/all_to_all | solution.py:101
  57.5 0.7 copy-start.2
  62.5 1.0 copy-start.15
  65.4 9.5 %copy-start.8 = (bf16[1,8,96,96]{3,2,0,1:T(8,128)(2,1)S(1)}, bf16[1,8,96,96]{3,2,0,1:T(8,128)(2,1)}, u32[]{:S(2)}) copy-start(bf16[1,8,96,96]{3,2,0,1:T(8,128)(2,1)} %get-tuple-element.26) | copy-start | bytes 442372
  65.4 9.5 %copy-start.9 = (bf16[1,8,96,96]{3,2,0,1:T(8,128)(2,1)S(1)}, bf16[1,8,96,96]{3,2,0,1:T(8,128)(2,1)}, u32[]{:S(2)}) copy-start(bf16[1,8,96,96]{3,2,0,1:T(8,128)(2,1)} %get-tuple-element.27) | copy-start | bytes 442372
  65.4 9.5 %copy-start.10 = (bf16[1,8,96,96]{3,2,0,1:T(8,128)(2,1)S(1)}, bf16[1,8,96,96]{3,2,0,1:T(8,128)(2,1)}, u32[]{:S(2)}) copy-start(bf16[1,8,96,96]{3,2,0,1:T(8,128)(2,1)} %get-tuple-element.28) | copy-start | bytes 442372
  68.5 7.5 %copy-start.11 = (bf16[1,8,96,96]{3,2,0,1:T(8,128)(2,1)S(1)}, bf16[1,8,96,96]{3,2,0,1:T(8,128)(2,1)}, u32[]{:S(2)}) copy-start(bf16[1,8,96,96]{3,2,0,1:T(8,128)(2,1)} %get-tuple-element.31) | copy-start | bytes 442372
  68.5 7.5 %copy-start.12 = (bf16[1,8,96,96]{3,2,0,1:T(8,128)(2,1)S(1)}, bf16[1,8,96,96]{3,2,0,1:T(8,128)(2,1)}, u32[]{:S(2)}) copy-start(bf16[1,8,96,96]{3,2,0,1:T(8,128)(2,1)} %get-tuple-element.32) | copy-start | bytes 442372
  68.5 7.5 %copy-start.13 = (bf16[1,8,96,96]{3,2,0,1:T(8,128)(2,1)S(1)}, bf16[1,8,96,96]{3,2,0,1:T(8,128)(2,1)}, u32[]{:S(2)}) copy-start(bf16[1,8,96,96]{3,2,0,1:T(8,128)(2,1)} %get-tuple-element.33) | copy-start | bytes 442372
  68.5 16.5 %all-to-all-start.5 = ((bf16[16,2,9216]{2,1,0:T(2,128)(2,1)}), bf16[16,2,9216]{2,1,0:T(2,128)(2,1)}, u32[]{:S(2)}, u32[]{:S(2)}) async-start(bf16[16,2,9216]{2,1,0:T(2,128)(2,1)} %reshape.319), calls=%async_computation.5 | async-start | bytes 1179648 | tf_op jit(solution)/shard_map/all_to_all | solution.py:101
  80.6 1.6 copy-start.25
  80.6 1.6 copy-start.27
  89.7 2.9 copy-start.26
  89.7 2.9 copy-start.28
  89.7 2.9 copy-start.32
  92.6 1.2 copy-start.1
  94.8 1.7 copy-start.7
  94.8 1.7 copy-start.19
  94.8 1.6 copy-start.20
  96.5 1.3 copy-start.17
  96.5 1.3 copy-start.18
  97.8 0.9 copy-start.5
  98.7 1.2 copy-start.23
  98.7 1.2 copy-start.24
  101.3 7.6 %copy-start.3 = (bf16[2,8,96,96]{3,2,0,1:T(8,128)(2,1)S(1)}, bf16[2,8,96,96]{3,2,0,1:T(8,128)(2,1)}, u32[]{:S(2)}) copy-start(bf16[2,8,96,96]{3,2,0,1:T(8,128)(2,1)} %copy-done.2) | copy-start | bytes 884740
  104.4 17.0 %all-to-all-start.6 = ((bf16[16,2,9216]{2,1,0:T(2,128)(2,1)}), bf16[16,2,9216]{2,1,0:T(2,128)(2,1)S(1)}, u32[]{:S(2)}, u32[]{:S(2)}) async-start(bf16[16,2,9216]{2,1,0:T(2,128)(2,1)} %reshape.321), calls=%async_computation.6 | async-start | bytes 1179648 | tf_op jit(solution)/shard_map/all_to_all | solution.py:113
  111.8 1.2 copy-start.6
  121.4 17.3 %all-to-all-start.2 = ((bf16[16,2,9216]{2,1,0:T(2,128)(2,1)}), bf16[16,2,9216]{2,1,0:T(2,128)(2,1)}, u32[]{:S(2)}, u32[]{:S(2)}) async-start(bf16[16,2,9216]{2,1,0:T(2,128)(2,1)} %reshape.313), calls=%async_computation.2 | async-start | bytes 1179648 | tf_op jit(solution)/shard_map/all_to_all | solution.py:113
  127.2 478.5 %all-reduce.3.cloned.1.call-start = ((), (), s32[]{:S(2)}) async-start(), calls=%async_computation.8 | async-start | bytes 3145728 | tf_op jit(solution)/shard_map/psum | solution.py:141
  131.0 1.2 copy-start.16
  138.7 470.5 %all-to-all-start.7 = ((bf16[16,2,9216]{2,1,0:T(2,128)(2,1)}), bf16[16,2,9216]{2,1,0:T(2,128)(2,1)}, u32[]{:S(2)}, u32[]{:S(2)}) async-start(bf16[16,2,9216]{2,1,0:T(2,128)(2,1)} %reshape.323), calls=%async_computation.7 | async-start | bytes 1179648 | tf_op jit(solution)/shard_map/all_to_all | solution.py:104
  605.7 2.4 copy-start.4
  609.2 17.9 %all-to-all-start.3 = ((bf16[16,2,9216]{2,1,0:T(2,128)(2,1)}), bf16[16,2,9216]{2,1,0:T(2,128)(2,1)}, u32[]{:S(2)}, u32[]{:S(2)}) async-start(bf16[16,2,9216]{2,1,0:T(2,128)(2,1)} %reshape.315), calls=%async_computation.3 | async-start | bytes 1179648 | tf_op jit(solution)/shard_map/all_to_all | solution.py:104
Sparse Core Ops, SparseCore 0:
  133.9 471.6 all-reduce.2
where the time goes:
time: 652 us; the launch traced here: 644 us
  waiting for transfers between devices  458 us (70%)
  local copies, waits for them, and re-layouts  88.6 us (14%)
  starting transfers between devices  52 us (8%)
  other arithmetic  17.4 us (3%)
  between operations  15.2 us (2%)
  matrix products  12.2 us (2%)
    psum x1, waiting for transfers between devices, on_device(): first_grad, second_grad = lax.psum((first_term, second_term), ('dp', 'lon'))  451 us
    unnamed x90, local copies, waits for them, and re-layouts  52.7 us
    all_to_all x2, starting transfers between devices, to_spectrum(): lax.all_to_all(grid_rows, 'lon', split_axis=2, concat_axis=0, tiled=True)  16.1 us
    all_to_all x2, starting transfers between devices, modes_to_lines(): lax.all_to_all(local_idft(all_modes), 'lon', split_axis=0, concat_axis=2,...  13.2 us
  transfers between devices with their start and end apart: 9, of which 4 were waited for; matrix products, arithmetic and copies ran while one was open for 13% of the time, Pallas kernels for 0%

commit v1 on v0

--- a/solution.py
+++ b/solution.py
@@ -138,7 +138,7 @@
     sample_count = lax.axis_size("dp")
     second_term = block_outer(act, dual) / sample_count
     first_term = block_outer(spectrum, pre) / sample_count
-    first_grad, second_grad = lax.psum((first_term, second_term), ("dp", "lon"))
+    first_grad, second_grad = lax.psum(lax.psum((first_term, second_term), "lon"), "dp")
     return (layer_out[None], field_grad[None], first_grad, second_grad)
 
 

time: 652 us -> 612 us (0.939)
  the two profiles are of different devices: /device:TPU:1 before, /device:TPU:8 now
where the time goes in v1:
time: 612 us; the launch traced here: 604 us
  waiting for transfers between devices  412 us (67%)
  local copies, waits for them, and re-layouts  89.6 us (15%)
  starting transfers between devices  54.3 us (9%)
  other arithmetic  17.8 us (3%)
  between operations  15.3 us (2%)
  matrix products  14.4 us (2%)
    psum x1, waiting for transfers between devices, on_device(): lax.psum(lax.psum((first_term, second_term), 'lon'), 'dp')  307 us
    psum x1, waiting for transfers between devices, on_device(): lax.psum((first_term, second_term), 'lon')  101 us
    unnamed x98, local copies, waits for them, and re-layouts  52 us
    all_to_all x2, starting transfers between devices, to_spectrum(): lax.all_to_all(grid_rows, 'lon', split_axis=2, concat_axis=0, tiled=True)  16.8 us
    all_to_all x2, starting transfers between devices, to_cells(): lax.all_to_all(spec_rows, 'lon', split_axis=3, concat_axis=0, tiled=True)  12.5 us
    all_to_all x2, starting transfers between devices, lines_to_modes(): lax.all_to_all(local_dft(all_lines), 'lon', split_axis=0, concat_axis=3,...  12.3 us
  transfers between devices with their start and end apart: 10, of which 5 were waited for; matrix products, arithmetic and copies ran while one was open for 15% of the time, Pallas kernels for 0%

profile of v1, /device:TPU:8, one launch (start us, length us, event | category | flops | bytes accessed | tf_op | source)
XLA Modules:
  0.0 603.5 jit_solution(5722045798979228778)
XLA Ops:
  7.2 2.0 copy.123
  9.3 3.1 reshape.309
  12.4 10.0 %all-to-all-start = ((bf16[16,2,9216]{2,1,0:T(2,128)(2,1)}), bf16[16,2,9216]{2,1,0:T(2,128)(2,1)}, u32[]{:S(2)}, u32[]{:S(2)}) async-start(bf16[16,2,9216]{2,1,0:T(2,128)(2,1)} %reshape.309), calls=%async_computation | async-start | bytes 1179648 | tf_op jit(solution)/shard_map/all_to_all | solution.py:108
  22.3 1.1 copy.137
  23.5 3.1 reshape.317
  29.0 2.4 all-to-all-done
  31.4 6.8 %all-to-all-start.4 = ((bf16[16,2,9216]{2,1,0:T(2,128)(2,1)}), bf16[16,2,9216]{2,1,0:T(2,128)(2,1)}, u32[]{:S(2)}, u32[]{:S(2)}) async-start(bf16[16,2,9216]{2,1,0:T(2,128)(2,1)} %reshape.317), calls=%async_computation.4 | async-start | bytes 1179648 | tf_op jit(solution)/shard_map/all_to_all | solution.py:108
  39.8 2.4 reshape.310
  42.2 1.0 copy.124
  43.3 1.0 copy.125
  44.8 1.4 copy.126
  46.2 3.1 reshape.311
  49.3 6.4 %all-to-all-start.1 = ((bf16[16,2,9216]{2,1,0:T(2,128)(2,1)}), bf16[16,2,9216]{2,1,0:T(2,128)(2,1)}, u32[]{:S(2)}, u32[]{:S(2)}) async-start(bf16[16,2,9216]{2,1,0:T(2,128)(2,1)} %reshape.311), calls=%async_computation.1 | async-start | bytes 1179648 | tf_op jit(solution)/shard_map/all_to_all | solution.py:101
  58.0 2.4 reshape.318
  60.4 1.0 copy.138
  61.5 1.0 copy.139
  63.0 1.4 copy.140
  64.4 3.1 reshape.319
  67.5 5.9 all-to-all-start.5
  73.9 1.1 maximum_bitcast_fusion.6
  75.0 1.1 maximum_bitcast_fusion.7
  76.0 2.4 reshape.312
  78.5 1.0 copy.127
  79.5 1.6 reshape.275
  82.4 2.4 reshape.320
  84.9 2.2 copy.141
  87.1 2.9 reshape.288
  91.7 1.4 fusion.59
  93.1 1.3 fusion.6
  97.3 1.2 fusion.41
  98.5 2.5 copy.148
  101.0 3.1 reshape.321
  104.1 6.7 %all-to-all-start.6 = ((bf16[16,2,9216]{2,1,0:T(2,128)(2,1)}), bf16[16,2,9216]{2,1,0:T(2,128)(2,1)}, u32[]{:S(2)}, u32[]{:S(2)}) async-start(bf16[16,2,9216]{2,1,0:T(2,128)(2,1)} %reshape.321), calls=%async_computation.6 | async-start | bytes 1179648 | tf_op jit(solution)/shard_map/all_to_all | solution.py:113
  110.9 1.7 fusion.37
  113.8 1.2 fusion.40
  115.0 3.0 convolution_bitcast_fusion
  118.0 2.5 copy.132
  120.5 3.1 reshape.313
  123.7 1.5 fusion.69
  125.2 5.8 all-to-all-start.2
  133.2 2.4 reshape.322
  135.7 1.2 copy.149
  136.9 1.5 fusion.30
  138.4 1.8 copy.151
  140.2 3.1 reshape.323
  143.3 5.7 all-to-all-start.7
  149.1 2.4 reshape.314
  151.5 1.2 copy.133
  152.7 1.5 fusion.27
  154.2 1.8 copy.135
  156.1 3.1 reshape.315
  159.2 1.6 all-to-all-done.7
  160.8 6.5 %all-to-all-start.3 = ((bf16[16,2,9216]{2,1,0:T(2,128)(2,1)}), bf16[16,2,9216]{2,1,0:T(2,128)(2,1)}, u32[]{:S(2)}, u32[]{:S(2)}) async-start(bf16[16,2,9216]{2,1,0:T(2,128)(2,1)} %reshape.315), calls=%async_computation.3 | async-start | bytes 1179648 | tf_op jit(solution)/shard_map/all_to_all | solution.py:104
  167.6 2.5 reshape.324
  170.0 101.2 %all-reduce.7.cloned.1.call-done = (f32[2,8,96,96]{2,3,1,0:T(8,128)}, f32[2,8,96,96]{2,3,1,0:T(8,128)}) async-done(((f32[2,8,96,96]{2,3,1,0:T(8,128)}, f32[2,8,96,96]{2,3,1,0:T(8,128)}), (f32[2,8,96,96]{2,3,1,0:T(8,128)}, f32[2,8,96,96]{2,3,1,0:T(8,128)})) %all-reduce.7.cloned.1.call-update) | async-done | bytes 1179664 | tf_op jit(solution)/shard_map/psum | solution.py:141
  271.6 1.8 copy.152
  273.4 2.2 reshape.269
  275.6 2.4 reshape.316
  278.4 1.8 copy.136
  280.2 2.2 reshape.268
  282.5 2.5 add_convert_fusion
  285.9 306.9 %all-reduce.5.cloned.1.call-done = (f32[2,8,96,96]{2,3,1,0:T(8,128)}, f32[2,8,96,96]{2,3,1,0:T(8,128)}) async-done(((f32[2,8,96,96]{2,3,1,0:T(8,128)}, f32[2,8,96,96]{2,3,1,0:T(8,128)}), (f32[2,8,96,96]{2,3,1,0:T(8,128)}, f32[2,8,96,96]{2,3,1,0:T(8,128)})) %all-reduce.5.cloned.1.call-update) | async-done | bytes 1179664 | tf_op jit(solution)/shard_map/psum | solution.py:141
  592.7 2.4 copy.158
  595.1 1.1 copy.159
  (118 shorter events, 19.0 us)
Async XLA Ops:
  12.3 10.0 %copy-start.1 = (bf16[1,8,48,768]{3,2,1,0:T(8,128)(2,1)S(1)}, bf16[1,8,48,768]{3,2,1,0:T(8,128)(2,1)}, u32[]{:S(2)}) copy-start(bf16[1,8,48,768]{3,2,1,0:T(8,128)(2,1)} %param.5) | copy-start | bytes 1769476
  12.4 19.0 %all-to-all-start = ((bf16[16,2,9216]{2,1,0:T(2,128)(2,1)}), bf16[16,2,9216]{2,1,0:T(2,128)(2,1)}, u32[]{:S(2)}, u32[]{:S(2)}) async-start(bf16[16,2,9216]{2,1,0:T(2,128)(2,1)} %reshape.309), calls=%async_computation | async-start | bytes 1179648 | tf_op jit(solution)/shard_map/all_to_all | solution.py:108
  23.5 15.4 %copy-start.22 = (bf16[2,8,96,96]{3,2,1,0:T(8,128)(2,1)S(1)}, bf16[2,8,96,96]{3,2,1,0:T(8,128)(2,1)}, u32[]{:S(2)}) copy-start(bf16[2,8,96,96]{3,2,1,0:T(8,128)(2,1)} %param.6) | copy-start | bytes 884740
  31.4 17.9 %all-to-all-start.4 = ((bf16[16,2,9216]{2,1,0:T(2,128)(2,1)}), bf16[16,2,9216]{2,1,0:T(2,128)(2,1)}, u32[]{:S(2)}, u32[]{:S(2)}) async-start(bf16[16,2,9216]{2,1,0:T(2,128)(2,1)} %reshape.317), calls=%async_computation.4 | async-start | bytes 1179648 | tf_op jit(solution)/shard_map/all_to_all | solution.py:108
  43.3 1.0 copy-start.15
  46.1 9.6 %copy-start.32 = (bf16[48,1,48]{2,0,1:T(8,128)(2,1)S(1)}, bf16[48,1,48]{2,0,1:T(8,128)(2,1)}, u32[]{:S(2)}) copy-start(bf16[48,1,48]{2,0,1:T(8,128)(2,1)} %get-tuple-element.50) | copy-start | bytes 13828
  46.1 9.6 %copy-start.33 = (bf16[48,1,48]{2,0,1:T(8,128)(2,1)S(1)}, bf16[48,1,48]{2,0,1:T(8,128)(2,1)}, u32[]{:S(2)}) copy-start(bf16[48,1,48]{2,0,1:T(8,128)(2,1)} %get-tuple-element.51) | copy-start | bytes 13828
  46.2 9.6 %copy-start.34 = (bf16[48,1,48]{2,0,1:T(8,128)(2,1)S(1)}, bf16[48,1,48]{2,0,1:T(8,128)(2,1)}, u32[]{:S(2)}) copy-start(bf16[48,1,48]{2,0,1:T(8,128)(2,1)} %fusion.91) | copy-start | bytes 13828
  46.2 10.2 %copy-start.23 = (bf16[2,8,96,96]{3,2,1,0:T(8,128)(2,1)S(1)}, bf16[2,8,96,96]{3,2,1,0:T(8,128)(2,1)}, u32[]{:S(2)}) copy-start(bf16[2,8,96,96]{3,2,1,0:T(8,128)(2,1)} %param.7) | copy-start | bytes 884740
  49.3 18.2 %all-to-all-start.1 = ((bf16[16,2,9216]{2,1,0:T(2,128)(2,1)}), bf16[16,2,9216]{2,1,0:T(2,128)(2,1)}, u32[]{:S(2)}, u32[]{:S(2)}) async-start(bf16[16,2,9216]{2,1,0:T(2,128)(2,1)} %reshape.311), calls=%async_computation.1 | async-start | bytes 1179648 | tf_op jit(solution)/shard_map/all_to_all | solution.py:101
  56.4 0.8 copy-start.4
  61.5 1.0 copy-start.16
  64.3 9.5 %copy-start.9 = (bf16[1,8,96,96]{3,2,0,1:T(8,128)(2,1)S(1)}, bf16[1,8,96,96]{3,2,0,1:T(8,128)(2,1)}, u32[]{:S(2)}) copy-start(bf16[1,8,96,96]{3,2,0,1:T(8,128)(2,1)} %get-tuple-element.28) | copy-start | bytes 442372
  64.3 9.5 %copy-start.10 = (bf16[1,8,96,96]{3,2,0,1:T(8,128)(2,1)S(1)}, bf16[1,8,96,96]{3,2,0,1:T(8,128)(2,1)}, u32[]{:S(2)}) copy-start(bf16[1,8,96,96]{3,2,0,1:T(8,128)(2,1)} %get-tuple-element.29) | copy-start | bytes 442372
  64.3 9.5 %copy-start.11 = (bf16[1,8,96,96]{3,2,0,1:T(8,128)(2,1)S(1)}, bf16[1,8,96,96]{3,2,0,1:T(8,128)(2,1)}, u32[]{:S(2)}) copy-start(bf16[1,8,96,96]{3,2,0,1:T(8,128)(2,1)} %get-tuple-element.30) | copy-start | bytes 442372
  67.4 7.5 %copy-start.12 = (bf16[1,8,96,96]{3,2,0,1:T(8,128)(2,1)S(1)}, bf16[1,8,96,96]{3,2,0,1:T(8,128)(2,1)}, u32[]{:S(2)}) copy-start(bf16[1,8,96,96]{3,2,0,1:T(8,128)(2,1)} %get-tuple-element.33) | copy-start | bytes 442372
  67.4 7.5 %copy-start.13 = (bf16[1,8,96,96]{3,2,0,1:T(8,128)(2,1)S(1)}, bf16[1,8,96,96]{3,2,0,1:T(8,128)(2,1)}, u32[]{:S(2)}) copy-start(bf16[1,8,96,96]{3,2,0,1:T(8,128)(2,1)} %get-tuple-element.34) | copy-start | bytes 442372
  67.4 7.5 %copy-start.14 = (bf16[1,8,96,96]{3,2,0,1:T(8,128)(2,1)S(1)}, bf16[1,8,96,96]{3,2,0,1:T(8,128)(2,1)}, u32[]{:S(2)}) copy-start(bf16[1,8,96,96]{3,2,0,1:T(8,128)(2,1)} %get-tuple-element.35) | copy-start | bytes 442372
  67.5 15.0 %all-to-all-start.5 = ((bf16[16,2,9216]{2,1,0:T(2,128)(2,1)}), bf16[16,2,9216]{2,1,0:T(2,128)(2,1)}, u32[]{:S(2)}, u32[]{:S(2)}) async-start(bf16[16,2,9216]{2,1,0:T(2,128)(2,1)} %reshape.319), calls=%async_computation.5 | async-start | bytes 1179648 | tf_op jit(solution)/shard_map/all_to_all | solution.py:101
  79.5 1.6 copy-start.28
  79.5 1.6 copy-start.30
  87.1 2.9 copy-start.29
  87.1 2.9 copy-start.31
  87.1 2.9 copy-start.35
  90.0 1.2 copy-start.3
  91.2 1.9 copy-start.8
  91.7 1.4 copy-start.20
  91.7 1.4 copy-start.21
  94.4 1.3 copy-start.18
  94.4 1.3 copy-start.19
  96.1 1.2 copy-start.24
  96.1 1.2 copy-start.26
  101.0 9.8 %copy-start.5 = (bf16[2,8,96,96]{3,2,0,1:T(8,128)(2,1)S(1)}, bf16[2,8,96,96]{3,2,0,1:T(8,128)(2,1)}, u32[]{:S(2)}) copy-start(bf16[2,8,96,96]{3,2,0,1:T(8,128)(2,1)} %copy-done.4) | copy-start | bytes 884740
  104.1 21.1 %all-to-all-start.6 = ((bf16[16,2,9216]{2,1,0:T(2,128)(2,1)}), bf16[16,2,9216]{2,1,0:T(2,128)(2,1)}, u32[]{:S(2)}, u32[]{:S(2)}) async-start(bf16[16,2,9216]{2,1,0:T(2,128)(2,1)} %reshape.321), calls=%async_computation.6 | async-start | bytes 1179648 | tf_op jit(solution)/shard_map/all_to_all | solution.py:113
  112.6 1.2 copy-start.25
  112.6 1.2 copy-start.27
  112.6 1.2 copy-start.36
  123.7 7.5 %copy-start.6 = (f32[1,8,96,96]{2,3,1,0:T(8,128)S(1)}, f32[1,8,96,96]{2,3,1,0:T(8,128)}, u32[]{:S(2)}) copy-start(f32[1,8,96,96]{2,3,1,0:T(8,128)} %fusion.70) | copy-start | bytes 884740
  125.2 18.1 %all-to-all-start.2 = ((bf16[16,2,9216]{2,1,0:T(2,128)(2,1)}), bf16[16,2,9216]{2,1,0:T(2,128)(2,1)}, u32[]{:S(2)}, u32[]{:S(2)}) async-start(bf16[16,2,9216]{2,1,0:T(2,128)(2,1)} %reshape.313), calls=%async_computation.2 | async-start | bytes 1179648 | tf_op jit(solution)/shard_map/all_to_all | solution.py:113
  131.0 140.3 %all-reduce.7.cloned.1.call-start = ((), (), s32[]{:S(2)}) async-start(), calls=%async_computation.9 | async-start | bytes 3145728 | tf_op jit(solution)/shard_map/psum | solution.py:141
  135.6 1.2 copy-start.17
  143.3 17.4 %all-to-all-start.7 = ((bf16[16,2,9216]{2,1,0:T(2,128)(2,1)}), bf16[16,2,9216]{2,1,0:T(2,128)(2,1)}, u32[]{:S(2)}, u32[]{:S(2)}) async-start(bf16[16,2,9216]{2,1,0:T(2,128)(2,1)} %reshape.323), calls=%async_computation.7 | async-start | bytes 1179648 | tf_op jit(solution)/shard_map/all_to_all | solution.py:104
  160.8 114.9 %all-to-all-start.3 = ((bf16[16,2,9216]{2,1,0:T(2,128)(2,1)}), bf16[16,2,9216]{2,1,0:T(2,128)(2,1)}, u32[]{:S(2)}, u32[]{:S(2)}) async-start(bf16[16,2,9216]{2,1,0:T(2,128)(2,1)} %reshape.315), calls=%async_computation.3 | async-start | bytes 1179648 | tf_op jit(solution)/shard_map/all_to_all | solution.py:104
  167.3 425.5 %all-reduce.5.cloned.1.call-start = ((), (), s32[]{:S(2)}) async-start(), calls=%async_computation.8 | async-start | bytes 3145728 | tf_op jit(solution)/shard_map/psum | solution.py:141
  282.5 2.5 copy-start
  282.5 2.5 copy-start.2
  592.7 2.4 copy-start.7
Sparse Core Ops, SparseCore 0:
  135.3 135.8 all-reduce.6
  274.4 318.2 all-reduce.4
